TPU v7x, 256 devices: a whole 4x4x8 slice. The times are simulated.
256 devices in a mesh: sub: 32 (over x, z), col: 8 (over y, core).
Axes of the slice: x: 4, y: 4, z: 8, core: 2. Of those that a mesh axis runs over, the one named last changes fastest.
Arguments:
- trace_start: bfloat16 [32, 8, 1536, 128], P('sub', 'col'), may hold values from -6 to 6
- neumann_load: bfloat16 [32, 8, 1536, 128], P('sub', 'col'), may hold values from -6 to 6
- double_layer: bfloat16 [32, 8, 1536, 1536], P('sub', 'col'), may hold values from -0.15625 to 0.15625
- single_inverse: bfloat16 [32, 8, 1536, 1536], P('sub', 'col'), may hold values from -0.15625 to 0.15625
- interface_nodes: int32 [32, 8, 8, 128], P('sub', 'col'), may hold values from -1 to 1023, as said below
- node_mode: int32 [32, 8, 1536], P('sub', 'col'), may hold values from 0 to 63
- mode_weight: bfloat16 [32, 8, 1536], P('sub', 'col'), may hold values from 0.5 to 1.5
- coarse_inverse: bfloat16 [16384, 16384], P('sub', 'col'), may hold values from -0.005859375 to 0.005859375
Outputs:
- final_trace: bfloat16 [32, 8, 1536, 128], P('sub', 'col')
- final_residual: bfloat16 [32, 8, 1536, 128], P('sub', 'col')
Inputs may be any that keep to these rules, and one draw needn't show every extreme that they name: `interface_nodes`: entry k of block (s, d) is a boundary node of s, within nodes d * 128 to (d + 1) * 128 - 1, distinct within the block, and matches entry k of the neighbour's block for direction 7 - d; valid entries come first and the rest are -1; blocks toward outside the grid are all -1; blocks of directions 1, 3, 4, 6 have 128 / 2 to 128 valid entries, the others 1 to 16, and some block has 128.
All inputs are finite; a program needn't handle non-finite values.
Results may differ from a plain program's by a relative error of at most 0.019.
Values may be sent and summed in bfloat16 or wider, within the bound.
A program may use at most 64 MiB of HBM per device.

v0:
```python
import jax
import jax.numpy as jnp
from jax import lax
from jax.sharding import PartitionSpec as P

MODES = 64
ITERS = 3
DIRECTIONS = ((-1, -1), (-1, 0), (-1, 1), (0, -1), (0, 1), (1, -1), (1, 0), (1, 1))


def from_behind(value, axis, by):
    devices = lax.axis_size(axis)
    pairs = [(i, i + by) for i in range(devices) if 0 <= i + by < devices]
    return lax.ppermute(value, axis, pairs)


def deliver_single(outgoing):
    arrivals = []
    for toward in range(8):
        row_step, col_step = DIRECTIONS[toward]
        message = outgoing[7 - toward]
        if row_step != 0:
            message = from_behind(message, "sub", -row_step)
        if col_step != 0:
            message = from_behind(message, "col", -col_step)
        arrivals.append(message)
    return jnp.stack(arrivals)


def local(
    trace_start,
    neumann_load,
    double_layer,
    single_inverse,
    interface_nodes,
    node_mode,
    mode_weight,
    coarse_inverse,
):
    trace_now = trace_start[0, 0]
    load_block = neumann_load[0, 0].astype(jnp.float32)
    kernel = double_layer[0, 0]
    inverse = single_inverse[0, 0]
    node_count = kernel.shape[0]
    interface = interface_nodes[0, 0]
    slot_count = interface.shape[1]
    band_rows = 8 * slot_count
    local_index = interface - (jnp.arange(8, dtype=jnp.int32) * slot_count)[:, None]
    selector = (
        local_index[:, :, None] == jnp.arange(slot_count, dtype=jnp.int32)[None, None, :]
    ).astype(jnp.bfloat16)
    mode_basis = jnp.where(
        node_mode[0, 0][None, :] == jnp.arange(MODES, dtype=jnp.int32)[:, None],
        mode_weight[0, 0][None, :],
        jnp.zeros((), jnp.bfloat16),
    )
    rhs_count = trace_now.shape[1]
    residual = trace_now
    rest_zeros = jnp.zeros((node_count - band_rows, rhs_count), jnp.float32)
    for iteration in range(ITERS):
        mixed_trace = (
            0.5 * trace_now.astype(jnp.float32)
            + jnp.dot(kernel, trace_now, preferred_element_type=jnp.float32)
        ).astype(jnp.bfloat16)
        flux_now = jnp.dot(inverse, mixed_trace, preferred_element_type=jnp.float32).astype(
            jnp.bfloat16
        )
        banded = flux_now[:band_rows].reshape(8, slot_count, rhs_count)
        outgoing = jnp.einsum(
            "dpq,dqr->dpr", selector, banded, preferred_element_type=jnp.float32
        ).astype(jnp.bfloat16)
        received = deliver_single(outgoing)
        placed = jnp.einsum(
            "dpq,dpr->dqr", selector, received, preferred_element_type=jnp.float32
        ).reshape(band_rows, rhs_count)
        assembled = flux_now.astype(jnp.float32) + jnp.concatenate([placed, rest_zeros], axis=0)
        residual = (load_block - assembled).astype(jnp.bfloat16)
        residual = lax.optimization_barrier(residual)
        coarse_rhs = jnp.dot(mode_basis, residual, preferred_element_type=jnp.float32).astype(
            jnp.bfloat16
        )
        partial_value = jnp.dot(
            coarse_inverse,
            lax.all_gather(coarse_rhs, "sub", axis=0, tiled=True),
            preferred_element_type=jnp.float32,
        )
        coarse_out = lax.psum_scatter(
            partial_value.astype(jnp.bfloat16), "col", scatter_dimension=0, tiled=True
        )
        correction = lax.dot_general(
            mode_basis, coarse_out, (((0,), (0,)), ((), ())), preferred_element_type=jnp.float32
        )
        trace_now = (
            trace_now.astype(jnp.float32) + 0.25 * residual.astype(jnp.float32) + correction
        ).astype(jnp.bfloat16)
    return (trace_now[None, None], residual[None, None])


def solution(mesh):
    placed = (
        P("sub", "col", None, None),
        P("sub", "col", None, None),
        P("sub", "col", None, None),
        P("sub", "col", None, None),
        P("sub", "col", None, None),
        P("sub", "col", None),
        P("sub", "col", None),
        P("sub", "col"),
    )
    return jax.shard_map(
        local,
        mesh=mesh,
        in_specs=placed,
        out_specs=(P("sub", "col", None, None), P("sub", "col", None, None)),
        check_vma=False,
    )
```

profile of v0, /device:TPU:2, one launch (start us, length us, event | category | flops | bytes accessed | tf_op | source)
XLA Modules:
  0.0 430.3 jit_solution(12199868396667985276)
XLA Ops:
  8.6 7.1 %fusion.54 = bf16[1536,128]{0,1:T(8,128)(2,1)S(1)} fusion(bf16[1,1,1536,1536]{3,2,1,0:T(8,128)(2,1)} %param.11, bf16[1,1,1536,1536]{3,2,1,0:T(8,128)(2,1)} %param.10, bf16[1,1,1536,128]{3,2,1,0:T(8,128)(2,1)} %param.8, bf16[1,1,1536,128]{2,3,1,0:T(8,128)(2,1)S(1)} %copy.26), kind=kOutput, calls=%fused_computation.31 | convolution fusion | flops 1208942592 | bytes 10616832 | tf_op jit(solution)/shard_map/dot_general | solution.py:65
  16.3 3.8 collective-permute-start
  20.2 5.9 %collective-permute-done = bf16[128,128]{1,0:T(8,128)(2,1)} collective-permute-done((bf16[128,128]{1,0:T(8,128)(2,1)S(1)}, bf16[128,128]{1,0:T(8,128)(2,1)}, u32[]{:S(2)}, u32[]{:S(2)}) %collective-permute-start) | collective-permute-done | bytes 32800 | tf_op jit(solution)/shard_map/ppermute | solution.py:14
  27.9 3.9 collective-permute-start.10
  56.2 3.8 collective-permute-start.8
  66.3 47.7 %all_gather.9 = bf16[2048,128]{1,0:T(8,128)(2,1)S(1)} all-gather(bf16[64,128]{1,0:T(8,128)(2,1)S(1)} %convolution_convert_fusion.8), channel_id=1, replica_groups=mesh['sub'=32,'col'=8] {'sub'}, dimensions={0}, use_global_device_ids=true | all-gather | bytes 540672 | tf_op jit(solution)/shard_map/all_gather | solution.py:84
  115.7 33.5 %reduce-scatter.10.cloned.1.call-done = bf16[64,128]{1,0:T(8,128)(2,1)} async-done(((bf16[512,128]{1,0:T(8,128)(2,1)}), bf16[64,128]{1,0:T(8,128)(2,1)}) %reduce-scatter.10.cloned.1.call-update) | async-done | bytes 16400
  150.5 6.9 %fusion.51 = bf16[1536,128]{0,1:T(8,128)(2,1)S(1)} fusion(bf16[1,1,1536,1536]{3,2,1,0:T(8,128)(2,1)} %param.11, bf16[1536,128]{0,1:T(8,128)(2,1)S(1)} %fusion.27, bf16[1,1,1536,1536]{3,2,1,0:T(8,128)(2,1)} %param.10), kind=kOutput, calls=%fused_computation.30 | convolution fusion | flops 1208942592 | bytes 10223616 | tf_op jit(solution)/shard_map/dot_general | solution.py:65
  159.7 3.5 collective-permute-start.12
  163.2 4.4 %collective-permute-done.12 = bf16[128,128]{1,0:T(8,128)(2,1)S(1)} collective-permute-done((bf16[128,128]{1,0:T(8,128)(2,1)S(1)}, bf16[128,128]{1,0:T(8,128)(2,1)S(1)}, u32[]{:S(2)}, u32[]{:S(2)}) %collective-permute-start.12) | collective-permute-done | bytes 32800 | tf_op jit(solution)/shard_map/ppermute | solution.py:14
  168.9 3.1 collective-permute-start.22
  172.0 3.3 collective-permute-start.21
  175.3 3.3 collective-permute-start.19
  194.7 3.8 collective-permute-start.20
  204.7 47.6 %all_gather.10 = bf16[2048,128]{1,0:T(8,128)(2,1)S(1)} all-gather(bf16[64,128]{1,0:T(8,128)(2,1)S(1)} %convolution_convert_fusion.7), channel_id=1, replica_groups=mesh['sub'=32,'col'=8] {'sub'}, dimensions={0}, use_global_device_ids=true | all-gather | bytes 540672 | tf_op jit(solution)/shard_map/all_gather | solution.py:84
  254.1 31.7 %reduce-scatter.12.cloned.1.call-done = bf16[64,128]{1,0:T(8,128)(2,1)} async-done(((bf16[512,128]{1,0:T(8,128)(2,1)}), bf16[64,128]{1,0:T(8,128)(2,1)}) %reduce-scatter.12.cloned.1.call-update) | async-done | bytes 16400
  287.1 6.9 %fusion.48 = bf16[1536,128]{0,1:T(8,128)(2,1)S(1)} fusion(bf16[1,1,1536,1536]{3,2,1,0:T(8,128)(2,1)} %param.11, bf16[1536,128]{0,1:T(8,128)(2,1)S(1)} %fusion.28, bf16[1,1,1536,1536]{3,2,1,0:T(8,128)(2,1)} %param.10), kind=kOutput, calls=%fused_computation.29 | convolution fusion | flops 1208942592 | bytes 10223616 | tf_op jit(solution)/shard_map/dot_general | solution.py:65
  296.4 3.5 collective-permute-start.24
  299.8 4.5 %collective-permute-done.24 = bf16[128,128]{1,0:T(8,128)(2,1)S(1)} collective-permute-done((bf16[128,128]{1,0:T(8,128)(2,1)S(1)}, bf16[128,128]{1,0:T(8,128)(2,1)S(1)}, u32[]{:S(2)}, u32[]{:S(2)}) %collective-permute-start.24) | collective-permute-done | bytes 32800 | tf_op jit(solution)/shard_map/ppermute | solution.py:14
  308.6 3.4 collective-permute-start.33
  312.0 3.2 collective-permute-start.31
  331.4 3.8 collective-permute-start.32
  340.7 47.7 %all_gather.11 = bf16[2048,128]{1,0:T(8,128)(2,1)S(1)} all-gather(bf16[64,128]{1,0:T(8,128)(2,1)S(1)} %convolution_convert_fusion.6), channel_id=1, replica_groups=mesh['sub'=32,'col'=8] {'sub'}, dimensions={0}, use_global_device_ids=true | all-gather | bytes 540672 | tf_op jit(solution)/shard_map/all_gather | solution.py:84
  390.9 31.0 %reduce-scatter.14.cloned.1.call-done = bf16[64,128]{1,0:T(8,128)(2,1)} async-done(((bf16[512,128]{1,0:T(8,128)(2,1)}), bf16[64,128]{1,0:T(8,128)(2,1)}) %reduce-scatter.14.cloned.1.call-update) | async-done | bytes 16400
  (140 shorter events, 98.6 us)
Async XLA Ops:
  7.2 142.0 %reduce-scatter.10.cloned.1.call-start = ((), (), s32[]{:S(2)}) async-start(), calls=%async_computation.3 | async-start | bytes 147456
  16.3 9.7 %collective-permute-start = (bf16[128,128]{1,0:T(8,128)(2,1)S(1)}, bf16[128,128]{1,0:T(8,128)(2,1)}, u32[]{:S(2)}, u32[]{:S(2)}) collective-permute-start(bf16[128,128]{1,0:T(8,128)(2,1)S(1)} %get-tuple-element.29), channel_id=1, source_target_pairs={{0,8},{8,16},{16,24},{24,32},{32,40},{40,48},{48,56},{56,64},{64,7... | collective-permute-start | bytes 98312 | tf_op jit(solution)/shard_map/ppermute | solution.py:14
  26.1 16.5 %collective-permute-start.1 = (bf16[128,128]{1,0:T(8,128)(2,1)}, bf16[128,128]{1,0:T(8,128)(2,1)}, u32[]{:S(2)}, u32[]{:S(2)}) collective-permute-start(bf16[128,128]{1,0:T(8,128)(2,1)} %collective-permute-done), channel_id=1, source_target_pairs={{0,1},{1,2},{2,3},{3,4},{4,5},{5,6},{6,7},{8,9},{9,10},{10,11},{11... | collective-permute-start | bytes 98312 | tf_op jit(solution)/shard_map/ppermute | solution.py:14
  27.9 23.9 %collective-permute-start.10 = (bf16[128,128]{1,0:T(8,128)(2,1)S(1)}, bf16[128,128]{1,0:T(8,128)(2,1)}, u32[]{:S(2)}, u32[]{:S(2)}) collective-permute-start(bf16[128,128]{1,0:T(8,128)(2,1)S(1)} %get-tuple-element.22), channel_id=1, source_target_pairs={{8,0},{16,8},{24,16},{32,24},{40,32},{48,40},{56,48},{64,56},{72,6... | collective-permute-start | bytes 98312 | tf_op jit(solution)/shard_map/ppermute | solution.py:14
  31.8 29.2 %collective-permute-start.9 = (bf16[128,128]{1,0:T(8,128)(2,1)S(1)}, bf16[128,128]{1,0:T(8,128)(2,1)S(1)}, u32[]{:S(2)}, u32[]{:S(2)}) collective-permute-start(bf16[128,128]{1,0:T(8,128)(2,1)S(1)} %get-tuple-element.23), channel_id=1, source_target_pairs={{8,0},{16,8},{24,16},{32,24},{40,32},{48,40},{56,48},{64,56},{72,6... | collective-permute-start | bytes 98312 | tf_op jit(solution)/shard_map/ppermute | solution.py:14
  34.8 20.1 %collective-permute-start.7 = (bf16[128,128]{1,0:T(8,128)(2,1)S(1)}, bf16[128,128]{1,0:T(8,128)(2,1)}, u32[]{:S(2)}, u32[]{:S(2)}) collective-permute-start(bf16[128,128]{1,0:T(8,128)(2,1)S(1)} %get-tuple-element.24), channel_id=1, source_target_pairs={{8,0},{16,8},{24,16},{32,24},{40,32},{48,40},{56,48},{64,56},{72,6... | collective-permute-start | bytes 98312 | tf_op jit(solution)/shard_map/ppermute | solution.py:14
  37.7 8.6 %collective-permute-start.3 = (bf16[128,128]{1,0:T(8,128)(2,1)S(1)}, bf16[128,128]{1,0:T(8,128)(2,1)}, u32[]{:S(2)}, u32[]{:S(2)}) collective-permute-start(bf16[128,128]{1,0:T(8,128)(2,1)S(1)} %get-tuple-element.27), channel_id=1, source_target_pairs={{0,8},{8,16},{16,24},{24,32},{32,40},{40,48},{48,56},{56,64},{64,7... | collective-permute-start | bytes 98312 | tf_op jit(solution)/shard_map/ppermute | solution.py:14
  46.3 13.7 %collective-permute-start.6 = (bf16[128,128]{1,0:T(8,128)(2,1)S(1)}, bf16[128,128]{1,0:T(8,128)(2,1)S(1)}, u32[]{:S(2)}, u32[]{:S(2)}) collective-permute-start(bf16[128,128]{1,0:T(8,128)(2,1)S(1)} %get-tuple-element.25), channel_id=1, source_target_pairs={{1,0},{2,1},{3,2},{4,3},{5,4},{6,5},{7,6},{9,8},{10,9},{11,10},{12... | collective-permute-start | bytes 98312 | tf_op jit(solution)/shard_map/ppermute | solution.py:14
  51.8 8.2 %collective-permute-start.5 = (bf16[128,128]{1,0:T(8,128)(2,1)S(1)}, bf16[128,128]{1,0:T(8,128)(2,1)S(1)}, u32[]{:S(2)}, u32[]{:S(2)}) collective-permute-start(bf16[128,128]{1,0:T(8,128)(2,1)S(1)} %get-tuple-element.26), channel_id=1, source_target_pairs={{0,1},{1,2},{2,3},{3,4},{4,5},{5,6},{6,7},{8,9},{9,10},{10,11},{11... | collective-permute-start | bytes 98312 | tf_op jit(solution)/shard_map/ppermute | solution.py:14
  115.6 170.2 %reduce-scatter.12.cloned.1.call-start = ((), (), s32[]{:S(2)}) async-start(), calls=%async_computation.4 | async-start | bytes 147456
  167.6 13.5 %collective-permute-start.13 = (bf16[128,128]{1,0:T(8,128)(2,1)S(1)}, bf16[128,128]{1,0:T(8,128)(2,1)S(1)}, u32[]{:S(2)}, u32[]{:S(2)}) collective-permute-start(bf16[128,128]{1,0:T(8,128)(2,1)S(1)} %collective-permute-done.12), channel_id=1, source_target_pairs={{0,1},{1,2},{2,3},{3,4},{4,5},{5,6},{6,7},{8,9},{9,10},{10,11},{11... | collective-permute-start | bytes 98312 | tf_op jit(solution)/shard_map/ppermute | solution.py:14
  168.9 21.5 %collective-permute-start.22 = (bf16[128,128]{1,0:T(8,128)(2,1)S(1)}, bf16[128,128]{1,0:T(8,128)(2,1)S(1)}, u32[]{:S(2)}, u32[]{:S(2)}) collective-permute-start(bf16[128,128]{1,0:T(8,128)(2,1)S(1)} %get-tuple-element.14), channel_id=1, source_target_pairs={{8,0},{16,8},{24,16},{32,24},{40,32},{48,40},{56,48},{64,56},{72,6... | collective-permute-start | bytes 98312 | tf_op jit(solution)/shard_map/ppermute | solution.py:14
  172.0 27.4 %collective-permute-start.21 = (bf16[128,128]{1,0:T(8,128)(2,1)S(1)}, bf16[128,128]{1,0:T(8,128)(2,1)S(1)}, u32[]{:S(2)}, u32[]{:S(2)}) collective-permute-start(bf16[128,128]{1,0:T(8,128)(2,1)S(1)} %get-tuple-element.15), channel_id=1, source_target_pairs={{8,0},{16,8},{24,16},{32,24},{40,32},{48,40},{56,48},{64,56},{72,6... | collective-permute-start | bytes 98312 | tf_op jit(solution)/shard_map/ppermute | solution.py:14
  175.3 18.1 %collective-permute-start.19 = (bf16[128,128]{1,0:T(8,128)(2,1)S(1)}, bf16[128,128]{1,0:T(8,128)(2,1)S(1)}, u32[]{:S(2)}, u32[]{:S(2)}) collective-permute-start(bf16[128,128]{1,0:T(8,128)(2,1)S(1)} %get-tuple-element.16), channel_id=1, source_target_pairs={{8,0},{16,8},{24,16},{32,24},{40,32},{48,40},{56,48},{64,56},{72,6... | collective-permute-start | bytes 98312 | tf_op jit(solution)/shard_map/ppermute | solution.py:14
  186.6 11.9 %collective-permute-start.18 = (bf16[128,128]{1,0:T(8,128)(2,1)S(1)}, bf16[128,128]{1,0:T(8,128)(2,1)S(1)}, u32[]{:S(2)}, u32[]{:S(2)}) collective-permute-start(bf16[128,128]{1,0:T(8,128)(2,1)S(1)} %get-tuple-element.17), channel_id=1, source_target_pairs={{1,0},{2,1},{3,2},{4,3},{5,4},{6,5},{7,6},{9,8},{10,9},{11,10},{12... | collective-permute-start | bytes 98312 | tf_op jit(solution)/shard_map/ppermute | solution.py:14
  190.4 8.2 %collective-permute-start.17 = (bf16[128,128]{1,0:T(8,128)(2,1)S(1)}, bf16[128,128]{1,0:T(8,128)(2,1)S(1)}, u32[]{:S(2)}, u32[]{:S(2)}) collective-permute-start(bf16[128,128]{1,0:T(8,128)(2,1)S(1)} %get-tuple-element.18), channel_id=1, source_target_pairs={{0,1},{1,2},{2,3},{3,4},{4,5},{5,6},{6,7},{8,9},{9,10},{10,11},{11... | collective-permute-start | bytes 98312 | tf_op jit(solution)/shard_map/ppermute | solution.py:14
  253.9 168.0 %reduce-scatter.14.cloned.1.call-start = ((), (), s32[]{:S(2)}) async-start(), calls=%async_computation.5 | async-start | bytes 147456
  304.3 13.5 %collective-permute-start.25 = (bf16[128,128]{1,0:T(8,128)(2,1)S(1)}, bf16[128,128]{1,0:T(8,128)(2,1)S(1)}, u32[]{:S(2)}, u32[]{:S(2)}) collective-permute-start(bf16[128,128]{1,0:T(8,128)(2,1)S(1)} %collective-permute-done.24), channel_id=1, source_target_pairs={{0,1},{1,2},{2,3},{3,4},{4,5},{5,6},{6,7},{8,9},{9,10},{10,11},{11... | collective-permute-start | bytes 98312 | tf_op jit(solution)/shard_map/ppermute | solution.py:14
  305.6 21.5 %collective-permute-start.34 = (bf16[128,128]{1,0:T(8,128)(2,1)S(1)}, bf16[128,128]{1,0:T(8,128)(2,1)S(1)}, u32[]{:S(2)}, u32[]{:S(2)}) collective-permute-start(bf16[128,128]{1,0:T(8,128)(2,1)S(1)} %get-tuple-element.6), channel_id=1, source_target_pairs={{8,0},{16,8},{24,16},{32,24},{40,32},{48,40},{56,48},{64,56},{72,6... | collective-permute-start | bytes 98312 | tf_op jit(solution)/shard_map/ppermute | solution.py:14
  308.6 27.5 %collective-permute-start.33 = (bf16[128,128]{1,0:T(8,128)(2,1)S(1)}, bf16[128,128]{1,0:T(8,128)(2,1)S(1)}, u32[]{:S(2)}, u32[]{:S(2)}) collective-permute-start(bf16[128,128]{1,0:T(8,128)(2,1)S(1)} %get-tuple-element.7), channel_id=1, source_target_pairs={{8,0},{16,8},{24,16},{32,24},{40,32},{48,40},{56,48},{64,56},{72,6... | collective-permute-start | bytes 98312 | tf_op jit(solution)/shard_map/ppermute | solution.py:14
  312.0 18.1 %collective-permute-start.31 = (bf16[128,128]{1,0:T(8,128)(2,1)S(1)}, bf16[128,128]{1,0:T(8,128)(2,1)S(1)}, u32[]{:S(2)}, u32[]{:S(2)}) collective-permute-start(bf16[128,128]{1,0:T(8,128)(2,1)S(1)} %get-tuple-element.8), channel_id=1, source_target_pairs={{8,0},{16,8},{24,16},{32,24},{40,32},{48,40},{56,48},{64,56},{72,6... | collective-permute-start | bytes 98312 | tf_op jit(solution)/shard_map/ppermute | solution.py:14
  315.2 8.1 %collective-permute-start.27 = (bf16[128,128]{1,0:T(8,128)(2,1)S(1)}, bf16[128,128]{1,0:T(8,128)(2,1)S(1)}, u32[]{:S(2)}, u32[]{:S(2)}) collective-permute-start(bf16[128,128]{1,0:T(8,128)(2,1)S(1)} %get-tuple-element.11), channel_id=1, source_target_pairs={{0,8},{8,16},{16,24},{24,32},{32,40},{40,48},{48,56},{56,64},{64,7... | collective-permute-start | bytes 98312 | tf_op jit(solution)/shard_map/ppermute | solution.py:14
  323.3 11.9 %collective-permute-start.30 = (bf16[128,128]{1,0:T(8,128)(2,1)S(1)}, bf16[128,128]{1,0:T(8,128)(2,1)S(1)}, u32[]{:S(2)}, u32[]{:S(2)}) collective-permute-start(bf16[128,128]{1,0:T(8,128)(2,1)S(1)} %get-tuple-element.9), channel_id=1, source_target_pairs={{1,0},{2,1},{3,2},{4,3},{5,4},{6,5},{7,6},{9,8},{10,9},{11,10},{12... | collective-permute-start | bytes 98312 | tf_op jit(solution)/shard_map/ppermute | solution.py:14
  327.1 8.2 %collective-permute-start.29 = (bf16[128,128]{1,0:T(8,128)(2,1)S(1)}, bf16[128,128]{1,0:T(8,128)(2,1)S(1)}, u32[]{:S(2)}, u32[]{:S(2)}) collective-permute-start(bf16[128,128]{1,0:T(8,128)(2,1)S(1)} %get-tuple-element.10), channel_id=1, source_target_pairs={{0,1},{1,2},{2,3},{3,4},{4,5},{5,6},{6,7},{8,9},{9,10},{10,11},{11... | collective-permute-start | bytes 98312 | tf_op jit(solution)/shard_map/ppermute | solution.py:14
  (21 other events, 288.8 us)
Sparse Core Ops, SparseCore 0:
  115.8 33.4 reduce-scatter.9
  254.0 31.7 reduce-scatter.11
  390.1 31.7 reduce-scatter.13
where the time goes:
time: 432 us; the launch traced here: 430 us
  blocking collectives  143 us (33%)
  waiting for transfers between devices  125 us (29%)
  starting transfers between devices  92.6 us (21%)
  matrix products  31.9 us (7%)
  local copies, waits for them, and re-layouts  19.3 us (4%)
  between operations  14.6 us (3%)
  other arithmetic  4.39 us (1%)
    all_gather x3, blocking collectives, local(): lax.all_gather(coarse_rhs, 'sub', axis=0, tiled=True)  143 us
    unnamed x6, waiting for transfers between devices  96.2 us
    ppermute x36, starting transfers between devices, from_behind(): return lax.ppermute(value, axis, pairs)  92.3 us
    ppermute x36, waiting for transfers between devices, from_behind(): return lax.ppermute(value, axis, pairs)  28.5 us
    dot_general x3, matrix products, local(): jnp.dot(inverse, mixed_trace, preferred_element_type=jnp.float32)  21 us
    unnamed x40, local copies, waits for them, and re-layouts  9.05 us
  transfers between devices with their start and end apart: 39, of which 14 were waited for; matrix products, arithmetic and copies ran while one was open for 1% of the time, Pallas kernels for 0%

commit v1 on v0

--- a/solution.py
+++ b/solution.py
@@ -6,6 +6,27 @@
 MODES = 64
 ITERS = 3
 DIRECTIONS = ((-1, -1), (-1, 0), (-1, 1), (0, -1), (0, 1), (1, -1), (1, 0), (1, 1))
+
+
+def state_regions_now(body, axis_no):
+    formed = list(body.shape[1:])
+    formed[axis_no] *= body.shape[0]
+    b_next = jnp.moveaxis(body, 0, axis_no).reshape(formed)
+    return b_next
+
+
+def solve_field(buf, axis_name):
+    arr_next = buf[None]
+    n_shards = lax.axis_size(axis_name)
+    for to_i in range(n_shards.bit_length() - 1):
+        new = 1 << to_i
+        shaped = lax.ppermute(arr_next, axis_name, [(it, it ^ new) for it in range(n_shards)])
+        current_arr = jnp.stack([arr_next, shaped], axis=0)
+        everything = lax.axis_index(axis_name) >> to_i & 1
+        arr_next = jnp.where(everything == 0, current_arr, current_arr[::-1]).reshape(
+            -1, *buf.shape
+        )
+    return arr_next
 
 
 def from_behind(value, axis, by):
@@ -79,9 +100,15 @@
         coarse_rhs = jnp.dot(mode_basis, residual, preferred_element_type=jnp.float32).astype(
             jnp.bfloat16
         )
+
+        def members_all_wrap(incoming_x, content, dim_i):
+            x_next = solve_field(incoming_x, content)
+            left_arr = state_regions_now(x_next, dim_i)
+            return left_arr
+
         partial_value = jnp.dot(
             coarse_inverse,
-            lax.all_gather(coarse_rhs, "sub", axis=0, tiled=True),
+            members_all_wrap(coarse_rhs, "sub", 0),
             preferred_element_type=jnp.float32,
         )
         coarse_out = lax.psum_scatter(

time: 432 us -> 384 us (0.89)
  blocking collectives: 143 us -> 0 us
  waiting for transfers between devices: 125 us -> 205 us
  starting transfers between devices: 92.6 us -> 107 us
    all_gather x3 -> x0, blocking collectives: 143 us -> none  [local(): lax.all_gather(coarse_rhs, 'sub', axis=0, tiled=True)]
    ppermute x0 -> x15, waiting for transfers between devices: none -> 78.4 us  [solve_field(): lax.ppermute(arr_next, axis_name, [(it, it ^ new) for it in range(n_shard...]
    ppermute x0 -> x15, starting transfers between devices: none -> 14.6 us  [solve_field(): lax.ppermute(arr_next, axis_name, [(it, it ^ new) for it in range(n_shard...]
  transfers between devices with their start and end apart: 39 -> 54, of which waited for: 14 -> 29; matrix products, arithmetic and copies ran while one was open for 1% -> 1% of each run, Pallas kernels for 0% -> 0%
where the time goes in v1:
time: 384 us; the launch traced here: 382 us
  waiting for transfers between devices  205 us (53%)
  starting transfers between devices  107 us (28%)
  matrix products  31.9 us (8%)
  local copies, waits for them, and re-layouts  18.5 us (5%)
  between operations  14.8 us (4%)
  other arithmetic  5.47 us (1%)
    unnamed x6, waiting for transfers between devices  97.7 us
    ppermute x36, starting transfers between devices, from_behind(): return lax.ppermute(value, axis, pairs)  92.2 us
    ppermute x15, waiting for transfers between devices, solve_field(): lax.ppermute(arr_next, axis_name, [(it, it ^ new) for it in range(n_shard...  78.4 us
    ppermute x36, waiting for transfers between devices, from_behind(): return lax.ppermute(value, axis, pairs)  28.6 us
    dot_general x3, matrix products, local(): jnp.dot(inverse, mixed_trace, preferred_element_type=jnp.float32)  21 us
    ppermute x15, starting transfers between devices, solve_field(): lax.ppermute(arr_next, axis_name, [(it, it ^ new) for it in range(n_shard...  14.6 us
    unnamed x40, local copies, waits for them, and re-layouts  8.32 us
  transfers between devices with their start and end apart: 54, of which 29 were waited for; matrix products, arithmetic and copies ran while one was open for 1% of the time, Pallas kernels for 0%

profile of v1, /device:TPU:2, one launch (start us, length us, event | category | flops | bytes accessed | tf_op | source)
XLA Modules:
  0.0 382.2 jit_solution(10032373875493266310)
XLA Ops:
  8.6 7.1 %fusion.54 = bf16[1536,128]{0,1:T(8,128)(2,1)S(1)} fusion(bf16[1,1,1536,1536]{3,2,1,0:T(8,128)(2,1)} %param.11, bf16[1,1,1536,1536]{3,2,1,0:T(8,128)(2,1)} %param.10, bf16[1,1,1536,128]{3,2,1,0:T(8,128)(2,1)} %param.8, bf16[1,1,1536,128]{2,3,1,0:T(8,128)(2,1)S(1)} %copy.29), kind=kOutput, calls=%fused_computation.31 | convolution fusion | flops 1208942592 | bytes 10616832 | tf_op jit(solution)/shard_map/dot_general | solution.py:86
  20.2 5.9 %collective-permute-done = bf16[128,128]{1,0:T(8,128)(2,1)} collective-permute-done((bf16[128,128]{1,0:T(8,128)(2,1)S(1)}, bf16[128,128]{1,0:T(8,128)(2,1)}, u32[]{:S(2)}, u32[]{:S(2)}) %collective-permute-start) | collective-permute-done | bytes 32800 | tf_op jit(solution)/shard_map/ppermute | solution.py:35
  27.9 3.9 %collective-permute-start.10 = (bf16[128,128]{1,0:T(8,128)(2,1)S(1)}, bf16[128,128]{1,0:T(8,128)(2,1)}, u32[]{:S(2)}, u32[]{:S(2)}) collective-permute-start(bf16[128,128]{1,0:T(8,128)(2,1)S(1)} %get-tuple-element.22), channel_id=1, source_target_pairs={{8,0},{16,8},{24,16},{32,24},{40,32},{48,40},{56,48},{64,56},{72,6... | collective-permute-start | bytes 98312 | tf_op jit(solution)/shard_map/ppermute | solution.py:35
  70.3 5.3 %collective-permute-done.13 = bf16[2,64,128]{2,1,0:T(8,128)(2,1)S(1)} collective-permute-done((bf16[2,64,128]{2,1,0:T(8,128)(2,1)S(1)}, bf16[2,64,128]{2,1,0:T(8,128)(2,1)S(1)}, u32[]{:S(2)}, u32[]{:S(2)}) %collective-permute-start.13) | collective-permute-done | bytes 32800 | tf_op jit(solution)/shard_map/ppermute | solution.py:23
  76.6 7.4 %collective-permute-done.14 = bf16[4,64,128]{2,1,0:T(8,128)(2,1)S(1)} collective-permute-done((bf16[4,64,128]{2,1,0:T(8,128)(2,1)S(1)}, bf16[4,64,128]{2,1,0:T(8,128)(2,1)S(1)}, u32[]{:S(2)}, u32[]{:S(2)}) %collective-permute-start.14) | collective-permute-done | bytes 65568 | tf_op jit(solution)/shard_map/ppermute | solution.py:23
  84.2 4.9 %collective-permute-done.15 = bf16[8,64,128]{2,1,0:T(8,128)(2,1)S(1)} collective-permute-done((bf16[8,64,128]{2,1,0:T(8,128)(2,1)S(1)}, bf16[8,64,128]{2,1,0:T(8,128)(2,1)S(1)}, u32[]{:S(2)}, u32[]{:S(2)}) %collective-permute-start.15) | collective-permute-done | bytes 131104 | tf_op jit(solution)/shard_map/ppermute | solution.py:23
  92.0 5.2 %collective-permute-done.16 = bf16[16,64,128]{2,1,0:T(8,128)(2,1)S(1)} collective-permute-done((bf16[16,64,128]{2,1,0:T(8,128)(2,1)S(1)}, bf16[16,64,128]{2,1,0:T(8,128)(2,1)S(1)}, u32[]{:S(2)}, u32[]{:S(2)}) %collective-permute-start.16) | collective-permute-done | bytes 262176 | tf_op jit(solution)/shard_map/ppermute | solution.py:23
  99.1 34.6 %reduce-scatter.10.cloned.1.call-done = bf16[64,128]{1,0:T(8,128)(2,1)} async-done(((bf16[512,128]{1,0:T(8,128)(2,1)}), bf16[64,128]{1,0:T(8,128)(2,1)}) %reduce-scatter.10.cloned.1.call-update) | async-done | bytes 16400
  134.9 6.9 %fusion.51 = bf16[1536,128]{0,1:T(8,128)(2,1)S(1)} fusion(bf16[1,1,1536,1536]{3,2,1,0:T(8,128)(2,1)} %param.11, bf16[1536,128]{0,1:T(8,128)(2,1)S(1)} %fusion.27, bf16[1,1,1536,1536]{3,2,1,0:T(8,128)(2,1)} %param.10), kind=kOutput, calls=%fused_computation.30 | convolution fusion | flops 1208942592 | bytes 10223616 | tf_op jit(solution)/shard_map/dot_general | solution.py:86
  147.5 4.5 %collective-permute-done.17 = bf16[128,128]{1,0:T(8,128)(2,1)S(1)} collective-permute-done((bf16[128,128]{1,0:T(8,128)(2,1)S(1)}, bf16[128,128]{1,0:T(8,128)(2,1)S(1)}, u32[]{:S(2)}, u32[]{:S(2)}) %collective-permute-start.17) | collective-permute-done | bytes 32800 | tf_op jit(solution)/shard_map/ppermute | solution.py:35
  192.4 5.3 %collective-permute-done.30 = bf16[2,64,128]{2,1,0:T(8,128)(2,1)S(1)} collective-permute-done((bf16[2,64,128]{2,1,0:T(8,128)(2,1)S(1)}, bf16[2,64,128]{2,1,0:T(8,128)(2,1)S(1)}, u32[]{:S(2)}, u32[]{:S(2)}) %collective-permute-start.30) | collective-permute-done | bytes 32800 | tf_op jit(solution)/shard_map/ppermute | solution.py:23
  198.5 7.6 %collective-permute-done.31 = bf16[4,64,128]{2,1,0:T(8,128)(2,1)S(1)} collective-permute-done((bf16[4,64,128]{2,1,0:T(8,128)(2,1)S(1)}, bf16[4,64,128]{2,1,0:T(8,128)(2,1)S(1)}, u32[]{:S(2)}, u32[]{:S(2)}) %collective-permute-start.31) | collective-permute-done | bytes 65568 | tf_op jit(solution)/shard_map/ppermute | solution.py:23
  206.3 5.0 %collective-permute-done.32 = bf16[8,64,128]{2,1,0:T(8,128)(2,1)S(1)} collective-permute-done((bf16[8,64,128]{2,1,0:T(8,128)(2,1)S(1)}, bf16[8,64,128]{2,1,0:T(8,128)(2,1)S(1)}, u32[]{:S(2)}, u32[]{:S(2)}) %collective-permute-start.32) | collective-permute-done | bytes 131104 | tf_op jit(solution)/shard_map/ppermute | solution.py:23
  211.3 4.1 %collective-permute-start.33 = (bf16[16,64,128]{2,1,0:T(8,128)(2,1)S(1)}, bf16[16,64,128]{2,1,0:T(8,128)(2,1)S(1)}, u32[]{:S(2)}, u32[]{:S(2)}) collective-permute-start(bf16[16,64,128]{2,1,0:T(8,128)(2,1)S(1)} %bitcast.299), channel_id=1, source_target_pairs={{0,128},{8,136},{16,144},{24,152},{32,160},{40,168},{48,176},{56,1... | collective-permute-start | bytes 786440 | tf_op jit(solution)/shard_map/ppermute | solution.py:23
  215.5 4.4 %collective-permute-done.33 = bf16[16,64,128]{2,1,0:T(8,128)(2,1)S(1)} collective-permute-done((bf16[16,64,128]{2,1,0:T(8,128)(2,1)S(1)}, bf16[16,64,128]{2,1,0:T(8,128)(2,1)S(1)}, u32[]{:S(2)}, u32[]{:S(2)}) %collective-permute-start.33) | collective-permute-done | bytes 262176 | tf_op jit(solution)/shard_map/ppermute | solution.py:23
  221.7 32.0 %reduce-scatter.12.cloned.1.call-done = bf16[64,128]{1,0:T(8,128)(2,1)} async-done(((bf16[512,128]{1,0:T(8,128)(2,1)}), bf16[64,128]{1,0:T(8,128)(2,1)}) %reduce-scatter.12.cloned.1.call-update) | async-done | bytes 16400
  255.0 6.9 %fusion.48 = bf16[1536,128]{0,1:T(8,128)(2,1)S(1)} fusion(bf16[1,1,1536,1536]{3,2,1,0:T(8,128)(2,1)} %param.11, bf16[1536,128]{0,1:T(8,128)(2,1)S(1)} %fusion.28, bf16[1,1,1536,1536]{3,2,1,0:T(8,128)(2,1)} %param.10), kind=kOutput, calls=%fused_computation.29 | convolution fusion | flops 1208942592 | bytes 10223616 | tf_op jit(solution)/shard_map/dot_general | solution.py:86
  267.7 4.4 %collective-permute-done.34 = bf16[128,128]{1,0:T(8,128)(2,1)S(1)} collective-permute-done((bf16[128,128]{1,0:T(8,128)(2,1)S(1)}, bf16[128,128]{1,0:T(8,128)(2,1)S(1)}, u32[]{:S(2)}, u32[]{:S(2)}) %collective-permute-start.34) | collective-permute-done | bytes 32800 | tf_op jit(solution)/shard_map/ppermute | solution.py:35
  312.5 5.3 %collective-permute-done.47 = bf16[2,64,128]{2,1,0:T(8,128)(2,1)S(1)} collective-permute-done((bf16[2,64,128]{2,1,0:T(8,128)(2,1)S(1)}, bf16[2,64,128]{2,1,0:T(8,128)(2,1)S(1)}, u32[]{:S(2)}, u32[]{:S(2)}) %collective-permute-start.47) | collective-permute-done | bytes 32800 | tf_op jit(solution)/shard_map/ppermute | solution.py:23
  318.6 7.6 %collective-permute-done.48 = bf16[4,64,128]{2,1,0:T(8,128)(2,1)S(1)} collective-permute-done((bf16[4,64,128]{2,1,0:T(8,128)(2,1)S(1)}, bf16[4,64,128]{2,1,0:T(8,128)(2,1)S(1)}, u32[]{:S(2)}, u32[]{:S(2)}) %collective-permute-start.48) | collective-permute-done | bytes 65568 | tf_op jit(solution)/shard_map/ppermute | solution.py:23
  326.4 5.0 %collective-permute-done.49 = bf16[8,64,128]{2,1,0:T(8,128)(2,1)S(1)} collective-permute-done((bf16[8,64,128]{2,1,0:T(8,128)(2,1)S(1)}, bf16[8,64,128]{2,1,0:T(8,128)(2,1)S(1)}, u32[]{:S(2)}, u32[]{:S(2)}) %collective-permute-start.49) | collective-permute-done | bytes 131104 | tf_op jit(solution)/shard_map/ppermute | solution.py:23
  331.4 4.1 %collective-permute-start.50 = (bf16[16,64,128]{2,1,0:T(8,128)(2,1)S(1)}, bf16[16,64,128]{2,1,0:T(8,128)(2,1)S(1)}, u32[]{:S(2)}, u32[]{:S(2)}) collective-permute-start(bf16[16,64,128]{2,1,0:T(8,128)(2,1)S(1)} %bitcast.297), channel_id=1, source_target_pairs={{0,128},{8,136},{16,144},{24,152},{32,160},{40,168},{48,176},{56,1... | collective-permute-start | bytes 786440 | tf_op jit(solution)/shard_map/ppermute | solution.py:23
  335.6 4.4 %collective-permute-done.50 = bf16[16,64,128]{2,1,0:T(8,128)(2,1)S(1)} collective-permute-done((bf16[16,64,128]{2,1,0:T(8,128)(2,1)S(1)}, bf16[16,64,128]{2,1,0:T(8,128)(2,1)S(1)}, u32[]{:S(2)}, u32[]{:S(2)}) %collective-permute-start.50) | collective-permute-done | bytes 262176 | tf_op jit(solution)/shard_map/ppermute | solution.py:23
  342.7 31.1 %reduce-scatter.14.cloned.1.call-done = bf16[64,128]{1,0:T(8,128)(2,1)} async-done(((bf16[512,128]{1,0:T(8,128)(2,1)}), bf16[64,128]{1,0:T(8,128)(2,1)}) %reduce-scatter.14.cloned.1.call-update) | async-done | bytes 16400
  (197 shorter events, 154.6 us)
Async XLA Ops:
  7.2 126.4 %reduce-scatter.10.cloned.1.call-start = ((), (), s32[]{:S(2)}) async-start(), calls=%async_computation.3 | async-start | bytes 147456
  16.3 9.7 %collective-permute-start = (bf16[128,128]{1,0:T(8,128)(2,1)S(1)}, bf16[128,128]{1,0:T(8,128)(2,1)}, u32[]{:S(2)}, u32[]{:S(2)}) collective-permute-start(bf16[128,128]{1,0:T(8,128)(2,1)S(1)} %get-tuple-element.29), channel_id=1, source_target_pairs={{0,8},{8,16},{16,24},{24,32},{32,40},{40,48},{48,56},{56,64},{64,7... | collective-permute-start | bytes 98312 | tf_op jit(solution)/shard_map/ppermute | solution.py:35
  26.1 16.5 %collective-permute-start.1 = (bf16[128,128]{1,0:T(8,128)(2,1)}, bf16[128,128]{1,0:T(8,128)(2,1)}, u32[]{:S(2)}, u32[]{:S(2)}) collective-permute-start(bf16[128,128]{1,0:T(8,128)(2,1)} %collective-permute-done), channel_id=1, source_target_pairs={{0,1},{1,2},{2,3},{3,4},{4,5},{5,6},{6,7},{8,9},{9,10},{10,11},{11... | collective-permute-start | bytes 98312 | tf_op jit(solution)/shard_map/ppermute | solution.py:35
  27.9 23.9 %collective-permute-start.10 = (bf16[128,128]{1,0:T(8,128)(2,1)S(1)}, bf16[128,128]{1,0:T(8,128)(2,1)}, u32[]{:S(2)}, u32[]{:S(2)}) collective-permute-start(bf16[128,128]{1,0:T(8,128)(2,1)S(1)} %get-tuple-element.22), channel_id=1, source_target_pairs={{8,0},{16,8},{24,16},{32,24},{40,32},{48,40},{56,48},{64,56},{72,6... | collective-permute-start | bytes 98312 | tf_op jit(solution)/shard_map/ppermute | solution.py:35
  31.9 29.2 %collective-permute-start.9 = (bf16[128,128]{1,0:T(8,128)(2,1)S(1)}, bf16[128,128]{1,0:T(8,128)(2,1)S(1)}, u32[]{:S(2)}, u32[]{:S(2)}) collective-permute-start(bf16[128,128]{1,0:T(8,128)(2,1)S(1)} %get-tuple-element.23), channel_id=1, source_target_pairs={{8,0},{16,8},{24,16},{32,24},{40,32},{48,40},{56,48},{64,56},{72,6... | collective-permute-start | bytes 98312 | tf_op jit(solution)/shard_map/ppermute | solution.py:35
  34.8 20.1 %collective-permute-start.7 = (bf16[128,128]{1,0:T(8,128)(2,1)S(1)}, bf16[128,128]{1,0:T(8,128)(2,1)}, u32[]{:S(2)}, u32[]{:S(2)}) collective-permute-start(bf16[128,128]{1,0:T(8,128)(2,1)S(1)} %get-tuple-element.24), channel_id=1, source_target_pairs={{8,0},{16,8},{24,16},{32,24},{40,32},{48,40},{56,48},{64,56},{72,6... | collective-permute-start | bytes 98312 | tf_op jit(solution)/shard_map/ppermute | solution.py:35
  37.7 8.6 %collective-permute-start.3 = (bf16[128,128]{1,0:T(8,128)(2,1)S(1)}, bf16[128,128]{1,0:T(8,128)(2,1)}, u32[]{:S(2)}, u32[]{:S(2)}) collective-permute-start(bf16[128,128]{1,0:T(8,128)(2,1)S(1)} %get-tuple-element.27), channel_id=1, source_target_pairs={{0,8},{8,16},{16,24},{24,32},{32,40},{40,48},{48,56},{56,64},{64,7... | collective-permute-start | bytes 98312 | tf_op jit(solution)/shard_map/ppermute | solution.py:35
  46.3 13.7 %collective-permute-start.6 = (bf16[128,128]{1,0:T(8,128)(2,1)S(1)}, bf16[128,128]{1,0:T(8,128)(2,1)S(1)}, u32[]{:S(2)}, u32[]{:S(2)}) collective-permute-start(bf16[128,128]{1,0:T(8,128)(2,1)S(1)} %get-tuple-element.25), channel_id=1, source_target_pairs={{1,0},{2,1},{3,2},{4,3},{5,4},{6,5},{7,6},{9,8},{10,9},{11,10},{12... | collective-permute-start | bytes 98312 | tf_op jit(solution)/shard_map/ppermute | solution.py:35
  75.6 8.4 %collective-permute-start.14 = (bf16[4,64,128]{2,1,0:T(8,128)(2,1)S(1)}, bf16[4,64,128]{2,1,0:T(8,128)(2,1)S(1)}, u32[]{:S(2)}, u32[]{:S(2)}) collective-permute-start(bf16[4,64,128]{2,1,0:T(8,128)(2,1)S(1)} %bitcast.307), channel_id=1, source_target_pairs={{0,32},{8,40},{16,48},{24,56},{32,0},{40,8},{48,16},{56,24},{64,96... | collective-permute-start | bytes 196616 | tf_op jit(solution)/shard_map/ppermute | solution.py:23
  99.0 154.7 %reduce-scatter.12.cloned.1.call-start = ((), (), s32[]{:S(2)}) async-start(), calls=%async_computation.4 | async-start | bytes 147456
  152.0 13.5 %collective-permute-start.18 = (bf16[128,128]{1,0:T(8,128)(2,1)S(1)}, bf16[128,128]{1,0:T(8,128)(2,1)S(1)}, u32[]{:S(2)}, u32[]{:S(2)}) collective-permute-start(bf16[128,128]{1,0:T(8,128)(2,1)S(1)} %collective-permute-done.17), channel_id=1, source_target_pairs={{0,1},{1,2},{2,3},{3,4},{4,5},{5,6},{6,7},{8,9},{9,10},{10,11},{11... | collective-permute-start | bytes 98312 | tf_op jit(solution)/shard_map/ppermute | solution.py:35
  153.3 21.5 %collective-permute-start.27 = (bf16[128,128]{1,0:T(8,128)(2,1)S(1)}, bf16[128,128]{1,0:T(8,128)(2,1)S(1)}, u32[]{:S(2)}, u32[]{:S(2)}) collective-permute-start(bf16[128,128]{1,0:T(8,128)(2,1)S(1)} %get-tuple-element.14), channel_id=1, source_target_pairs={{8,0},{16,8},{24,16},{32,24},{40,32},{48,40},{56,48},{64,56},{72,6... | collective-permute-start | bytes 98312 | tf_op jit(solution)/shard_map/ppermute | solution.py:35
  156.3 27.5 %collective-permute-start.26 = (bf16[128,128]{1,0:T(8,128)(2,1)S(1)}, bf16[128,128]{1,0:T(8,128)(2,1)S(1)}, u32[]{:S(2)}, u32[]{:S(2)}) collective-permute-start(bf16[128,128]{1,0:T(8,128)(2,1)S(1)} %get-tuple-element.15), channel_id=1, source_target_pairs={{8,0},{16,8},{24,16},{32,24},{40,32},{48,40},{56,48},{64,56},{72,6... | collective-permute-start | bytes 98312 | tf_op jit(solution)/shard_map/ppermute | solution.py:35
  159.7 18.1 %collective-permute-start.24 = (bf16[128,128]{1,0:T(8,128)(2,1)S(1)}, bf16[128,128]{1,0:T(8,128)(2,1)S(1)}, u32[]{:S(2)}, u32[]{:S(2)}) collective-permute-start(bf16[128,128]{1,0:T(8,128)(2,1)S(1)} %get-tuple-element.16), channel_id=1, source_target_pairs={{8,0},{16,8},{24,16},{32,24},{40,32},{48,40},{56,48},{64,56},{72,6... | collective-permute-start | bytes 98312 | tf_op jit(solution)/shard_map/ppermute | solution.py:35
  171.0 11.9 %collective-permute-start.23 = (bf16[128,128]{1,0:T(8,128)(2,1)S(1)}, bf16[128,128]{1,0:T(8,128)(2,1)S(1)}, u32[]{:S(2)}, u32[]{:S(2)}) collective-permute-start(bf16[128,128]{1,0:T(8,128)(2,1)S(1)} %get-tuple-element.17), channel_id=1, source_target_pairs={{1,0},{2,1},{3,2},{4,3},{5,4},{6,5},{7,6},{9,8},{10,9},{11,10},{12... | collective-permute-start | bytes 98312 | tf_op jit(solution)/shard_map/ppermute | solution.py:35
  197.8 8.4 %collective-permute-start.31 = (bf16[4,64,128]{2,1,0:T(8,128)(2,1)S(1)}, bf16[4,64,128]{2,1,0:T(8,128)(2,1)S(1)}, u32[]{:S(2)}, u32[]{:S(2)}) collective-permute-start(bf16[4,64,128]{2,1,0:T(8,128)(2,1)S(1)} %bitcast.311), channel_id=1, source_target_pairs={{0,32},{8,40},{16,48},{24,56},{32,0},{40,8},{48,16},{56,24},{64,96... | collective-permute-start | bytes 196616 | tf_op jit(solution)/shard_map/ppermute | solution.py:23
  211.3 8.5 %collective-permute-start.33 = (bf16[16,64,128]{2,1,0:T(8,128)(2,1)S(1)}, bf16[16,64,128]{2,1,0:T(8,128)(2,1)S(1)}, u32[]{:S(2)}, u32[]{:S(2)}) collective-permute-start(bf16[16,64,128]{2,1,0:T(8,128)(2,1)S(1)} %bitcast.299), channel_id=1, source_target_pairs={{0,128},{8,136},{16,144},{24,152},{32,160},{40,168},{48,176},{56,1... | collective-permute-start | bytes 786440 | tf_op jit(solution)/shard_map/ppermute | solution.py:23
  221.7 152.1 %reduce-scatter.14.cloned.1.call-start = ((), (), s32[]{:S(2)}) async-start(), calls=%async_computation.5 | async-start | bytes 147456
  272.2 13.5 %collective-permute-start.35 = (bf16[128,128]{1,0:T(8,128)(2,1)S(1)}, bf16[128,128]{1,0:T(8,128)(2,1)S(1)}, u32[]{:S(2)}, u32[]{:S(2)}) collective-permute-start(bf16[128,128]{1,0:T(8,128)(2,1)S(1)} %collective-permute-done.34), channel_id=1, source_target_pairs={{0,1},{1,2},{2,3},{3,4},{4,5},{5,6},{6,7},{8,9},{9,10},{10,11},{11... | collective-permute-start | bytes 98312 | tf_op jit(solution)/shard_map/ppermute | solution.py:35
  273.5 21.5 %collective-permute-start.44 = (bf16[128,128]{1,0:T(8,128)(2,1)S(1)}, bf16[128,128]{1,0:T(8,128)(2,1)S(1)}, u32[]{:S(2)}, u32[]{:S(2)}) collective-permute-start(bf16[128,128]{1,0:T(8,128)(2,1)S(1)} %get-tuple-element.6), channel_id=1, source_target_pairs={{8,0},{16,8},{24,16},{32,24},{40,32},{48,40},{56,48},{64,56},{72,6... | collective-permute-start | bytes 98312 | tf_op jit(solution)/shard_map/ppermute | solution.py:35
  276.5 27.4 %collective-permute-start.43 = (bf16[128,128]{1,0:T(8,128)(2,1)S(1)}, bf16[128,128]{1,0:T(8,128)(2,1)S(1)}, u32[]{:S(2)}, u32[]{:S(2)}) collective-permute-start(bf16[128,128]{1,0:T(8,128)(2,1)S(1)} %get-tuple-element.7), channel_id=1, source_target_pairs={{8,0},{16,8},{24,16},{32,24},{40,32},{48,40},{56,48},{64,56},{72,6... | collective-permute-start | bytes 98312 | tf_op jit(solution)/shard_map/ppermute | solution.py:35
  279.9 18.1 %collective-permute-start.41 = (bf16[128,128]{1,0:T(8,128)(2,1)S(1)}, bf16[128,128]{1,0:T(8,128)(2,1)S(1)}, u32[]{:S(2)}, u32[]{:S(2)}) collective-permute-start(bf16[128,128]{1,0:T(8,128)(2,1)S(1)} %get-tuple-element.8), channel_id=1, source_target_pairs={{8,0},{16,8},{24,16},{32,24},{40,32},{48,40},{56,48},{64,56},{72,6... | collective-permute-start | bytes 98312 | tf_op jit(solution)/shard_map/ppermute | solution.py:35
  291.2 11.9 %collective-permute-start.40 = (bf16[128,128]{1,0:T(8,128)(2,1)S(1)}, bf16[128,128]{1,0:T(8,128)(2,1)S(1)}, u32[]{:S(2)}, u32[]{:S(2)}) collective-permute-start(bf16[128,128]{1,0:T(8,128)(2,1)S(1)} %get-tuple-element.9), channel_id=1, source_target_pairs={{1,0},{2,1},{3,2},{4,3},{5,4},{6,5},{7,6},{9,8},{10,9},{11,10},{12... | collective-permute-start | bytes 98312 | tf_op jit(solution)/shard_map/ppermute | solution.py:35
  331.4 8.5 %collective-permute-start.50 = (bf16[16,64,128]{2,1,0:T(8,128)(2,1)S(1)}, bf16[16,64,128]{2,1,0:T(8,128)(2,1)S(1)}, u32[]{:S(2)}, u32[]{:S(2)}) collective-permute-start(bf16[16,64,128]{2,1,0:T(8,128)(2,1)S(1)} %bitcast.297), channel_id=1, source_target_pairs={{0,128},{8,136},{16,144},{24,152},{32,160},{40,168},{48,176},{56,1... | collective-permute-start | bytes 786440 | tf_op jit(solution)/shard_map/ppermute | solution.py:23
  (36 other events, 395.4 us)
Sparse Core Ops, SparseCore 0:
  99.1 34.4 reduce-scatter.9
  221.8 31.8 reduce-scatter.11
  341.9 31.8 reduce-scatter.13
